TPU v7x, 512 devices: a whole 4x8x8 slice. The times are simulated.
512 devices in a mesh: row: 32 (over x, y), col: 16 (over z, core).
Axes of the slice: x: 4, y: 8, z: 8, core: 2. Of those that a mesh axis runs over, the one named last changes fastest.
Arguments:
- window: float32 [32, 2048, 16, 256], P('row', None, 'col'), may hold values from -7 to 8, as said below
Outputs:
- factored: float32 [32, 2048, 16, 256], P('row', None, 'col')
Inputs may be any that keep to these rules, and one draw needn't show every extreme that they name: `window`: entries above the diagonal are never read. The leading 2 * 128 by 256 block (lower triangle mirrored) is positive definite, with smallest eigenvalue 1 or more.
All inputs are finite; a program needn't handle non-finite values.
Results may differ from a plain program's by a relative error of at most 0.00028.
Values sent between devices are 32-bit elements; how exact they have to be, the bound alone decides.
A program may use at most 64 MiB of HBM per device.

v0:
```python
import jax
import jax.numpy as jnp
from jax import lax
from jax.sharding import PartitionSpec as P

NB = 128


def unmix_cols(gathered, col_count):
    height = gathered.shape[0]
    width = gathered.shape[1]
    return (
        gathered.reshape(height, col_count, width // col_count)
        .transpose(0, 2, 1)
        .reshape(height, width)
    )


def solve_rows(factor, rows_in):
    return jax.scipy.linalg.solve_triangular(factor, rows_in.T, lower=True).T


def body(window):
    blocks = window[0, :, 0, :]
    local_rows = blocks.shape[0]
    local_cols = blocks.shape[1]
    row_count = lax.axis_size("row")
    col_count = lax.axis_size("col")
    row_index = lax.axis_index("row")
    col_index = lax.axis_index("col")
    tile_height = NB // row_count
    tile_width = NB // col_count
    head_rows = local_cols * col_count // row_count
    groups = row_count // col_count
    for panel_step in range(2):
        first_col = panel_step * tile_width
        after_col = first_col + tile_width
        first_row = panel_step * tile_height
        tile_piece = blocks[first_row : first_row + tile_height, first_col:after_col]
        tile_wide = lax.all_gather(tile_piece, "col", axis=1, tiled=True)
        tile_full = lax.all_gather(tile_wide, "row", axis=0, tiled=True)
        tile_full = tile_full.reshape(row_count, tile_height, NB).transpose(1, 0, 2).reshape(NB, NB)
        diag_tile = unmix_cols(tile_full, col_count)
        symmetric = jnp.tril(diag_tile) + jnp.tril(diag_tile, -1).T
        factor = jnp.tril(jnp.linalg.cholesky(symmetric))
        panel_mine = blocks[:, first_col:after_col]
        gathered = lax.all_gather(panel_mine, "col", axis=1, tiled=True)
        solved = solve_rows(factor, unmix_cols(gathered, col_count))
        diag_rows = lax.dynamic_index_in_dim(
            factor.reshape(tile_height, row_count, NB), row_index, 1, False
        )
        panel_rows = jnp.concatenate(
            [jnp.zeros((first_row, NB), jnp.float32), diag_rows, solved[first_row + tile_height :]],
            0,
        )
        own_cols = lax.dynamic_index_in_dim(
            panel_rows.reshape(local_rows, tile_width, col_count), col_index, 2, False
        )
        sending = panel_rows[:head_rows]
        all_rows = lax.all_gather(sending, "row", axis=0, tiled=True)
        picked = lax.dynamic_index_in_dim(
            all_rows.reshape(groups, col_count, head_rows, NB), col_index, 1, False
        )
        col_rows = picked.transpose(1, 0, 2).reshape(local_cols, NB)
        update = jnp.dot(panel_rows, col_rows[after_col:].T, precision=lax.Precision.HIGHEST)
        trailing = blocks[:, after_col:] - update
        blocks = jnp.concatenate([blocks[:, :first_col], own_cols, trailing], 1)
    global_rows = jnp.arange(local_rows)[:, None] * row_count + row_index
    global_cols = jnp.arange(local_cols)[None, :] * col_count + col_index
    lower_mask = global_rows >= global_cols
    result = jnp.where(lower_mask, blocks, 0.0)
    return result[None, :, None, :]


def solution(mesh):
    in_specs = (P("row", None, "col", None),)
    out_specs = P("row", None, "col", None)
    return jax.shard_map(body, mesh=mesh, in_specs=in_specs, out_specs=out_specs, check_vma=False)
```

profile of v0, /device:TPU:14, one launch (start us, length us, event | category | flops | bytes accessed | tf_op | source)
XLA Modules:
  0.0 380.1 jit_solution(15478815313496594066)
XLA Ops:
  6.5 4.6 %copy.51 = f32[1,2048,1,256]{1,3,2,0:T(8,128)S(1)} copy(f32[1,2048,1,256]{3,2,1,0:T(1,128)} %param.4) | data formatting | bytes 4194304 | tf_op args[0]
  11.1 0.6 slice.65
  11.9 23.2 %all-gather = f32[16,8,4]{1,2,0:T(4,128)S(1)} all-gather(f32[1,8,4]{1,2,0:T(4,128)S(1)} %bitcast.136), channel_id=1, replica_groups=mesh['row'=32,'col'=16] {'col'}, dimensions={0}, use_global_device_ids=true | all-gather | bytes 2176 | tf_op jit(solution)/shard_map/all_gather | solution.py:40
  35.1 0.1 reshape.171
  35.2 48.2 %all-gather.1 = f32[32,4,128]{2,1,0:T(4,128)S(1)} all-gather(f32[1,4,128]{2,1,0:T(4,128)S(1)} %bitcast.137), channel_id=1, replica_groups=mesh['row'=32,'col'=16] {'row'}, dimensions={0}, use_global_device_ids=true | all-gather | bytes 67584 | tf_op jit(solution)/shard_map/all_gather | solution.py:41
  83.4 0.2 copy.54
  83.6 0.2 reshape_reshape.6
  83.7 0.1 copy.57
  83.9 0.1 bitcast_add_fusion.3
  83.9 0.1 copy.58
  84.1 11.7 %cholesky.44 = f32[128,128]{1,0:T(8,128)S(1)} custom-call(f32[128,128]{1,0:T(8,128)S(1)} %fusion.8), custom_call_target="Cholesky" | custom-call | tf_op jit(solution)/shard_map/jit(cholesky)/cholesky | solution.py:45
  95.8 0.1 copy.59
  95.9 0.1 select_reduce_fusion.1
  96.0 0.7 compare_reduce_fusion.1
  96.7 0.6 select_bitcast_fusion.1
  97.3 0.1 copy.62
  97.5 0.1 copy.66
  97.6 0.1 copy.63
  97.7 9.8 %custom-call.6 = f32[1,128,128]{1,2,0:T(8,128)S(1)} custom-call(f32[1,128,128]{2,1,0:T(8,128)S(1)} %copy.63), custom_call_target="InvertDiagBlocksLowerTriangular" | custom-call | tf_op jit(solution)/shard_map/jit(_solve_triangular)/triangular_solve | solution.py:20
  107.5 1.8 copy.64
  109.4 1.1 convolution_bitcast_fusion.1
  110.4 0.3 slice.66
  110.7 0.7 pad_maximum_fusion
  111.5 76.0 %all-gather.11.cloned.1.call-done = f32[4096,128]{0,1:T(8,128)} async-done(((f32[128,128]{0,1:T(8,128)}), f32[4096,128]{0,1:T(8,128)}) %all-gather.11.cloned.1.call-update) | async-done | bytes 2097168 | tf_op jit(solution)/shard_map/all_gather | solution.py:60
  187.6 2.0 copy.88
  189.5 0.1 constant_dynamic-slice_fusion.2
  189.7 0.1 copy.67
  189.8 1.9 convolution_subtract_fusion
  191.7 1.3 copy-done
  193.0 0.6 slice.70
  193.7 0.2 all-gather.15.cloned.1.call-start
  193.9 0.1 copy.75
  194.0 0.8 slice_bitcast_fusion
  194.8 0.1 copy.68
  194.9 18.1 %all-gather.2 = f32[16,8,4]{1,2,0:T(4,128)S(1)} all-gather(f32[1,8,4]{1,2,0:T(4,128)S(1)} %bitcast.138), channel_id=1, replica_groups=mesh['row'=32,'col'=16] {'col'}, dimensions={0}, use_global_device_ids=true | all-gather | bytes 2176 | tf_op jit(solution)/shard_map/all_gather | solution.py:40
  213.0 0.1 reshape.175
  213.1 46.1 %all-gather.3 = f32[32,4,128]{2,1,0:T(4,128)S(1)} all-gather(f32[1,4,128]{2,1,0:T(4,128)S(1)} %bitcast.139), channel_id=1, replica_groups=mesh['row'=32,'col'=16] {'row'}, dimensions={0}, use_global_device_ids=true | all-gather | bytes 67584 | tf_op jit(solution)/shard_map/all_gather | solution.py:41
  259.2 0.2 copy.70
  259.4 0.2 reshape_reshape.7
  259.6 0.1 copy.73
  259.7 0.1 bitcast_add_fusion.1
  259.8 0.1 copy.74
  259.9 11.7 %cholesky.55 = f32[128,128]{1,0:T(8,128)S(1)} custom-call(f32[128,128]{1,0:T(8,128)S(1)} %fusion.6), custom_call_target="Cholesky" | custom-call | tf_op jit(solution)/shard_map/jit(cholesky)/cholesky | solution.py:45
  271.6 0.6 compare_reduce_fusion
  272.3 0.6 select_bitcast_fusion
  272.8 9.8 %custom-call.7 = f32[1,128,128]{1,2,0:T(8,128)S(1)} custom-call(f32[1,128,128]{2,1,0:T(8,128)S(1)} %get-tuple-element.6), custom_call_target="InvertDiagBlocksLowerTriangular" | custom-call | tf_op jit(solution)/shard_map/jit(_solve_triangular)/triangular_solve | solution.py:20
  282.7 0.1 copy.80
  282.8 1.8 copy.77
  284.7 1.1 convolution_bitcast_fusion
  285.7 0.3 slice.71
  286.1 1.0 concatenate.45
  287.0 0.7 slice.73
  287.7 0.1 copy.83
  287.9 0.2 fusion.4
  288.2 0.1 copy.78
  288.3 0.6 copy.79
  288.9 0.7 concatenate.43
  289.7 75.8 %all-gather.15.cloned.1.call-done = f32[4096,128]{0,1:T(8,128)} async-done(((f32[128,128]{0,1:T(8,128)}), f32[4096,128]{0,1:T(8,128)}) %all-gather.15.cloned.1.call-update) | async-done | bytes 2097168 | tf_op jit(solution)/shard_map/all_gather | solution.py:60
  365.5 2.1 copy.89
  367.6 0.1 constant_dynamic-slice_fusion
  367.8 0.1 copy.81
  368.0 1.8 fusion
  369.8 0.2 maximum_select_fusion
  370.0 3.6 copy.82
  (37 shorter events, 0.6 us)
Async XLA Ops:
  6.5 101.0 %all-gather.9.cloned.1.call-start = ((), (), s32[]{:S(2)}) async-start(), calls=%async_computation | async-start | bytes 1114112 | tf_op jit(solution)/shard_map/all_gather | solution.py:47
  11.8 175.8 %all-gather.11.cloned.1.call-start = ((), (), s32[]{:S(2)}) async-start(), calls=%async_computation.1 | async-start | bytes 2162688 | tf_op jit(solution)/shard_map/all_gather | solution.py:60
  111.5 171.3 %all-gather.13.cloned.1.call-start = ((), (), s32[]{:S(2)}) async-start(), calls=%async_computation.2 | async-start | bytes 1114112 | tf_op jit(solution)/shard_map/all_gather | solution.py:47
  191.7 1.3 copy-start
  193.7 171.9 %all-gather.15.cloned.1.call-start = ((), (), s32[]{:S(2)}) async-start(), calls=%async_computation.3 | async-start | bytes 2162688 | tf_op jit(solution)/shard_map/all_gather | solution.py:60
  287.0 2.6 copy-start.2
  365.5 2.4 copy-start.1
  365.5 2.5 copy-start.3
Sparse Core Ops, SparseCore 0:
  11.9 46.4 all-gather.8
  111.6 75.8 all-gather.10
  193.8 41.1 all-gather.12
  287.9 77.6 all-gather.14
where the time goes:
time: 380 us
  waiting for transfers between devices  152 us (40%)
  blocking collectives  136 us (36%)
  other arithmetic  47.1 us (12%)
  local copies, waits for them, and re-layouts  25.8 us (7%)
  between operations  13.6 us (4%)
  matrix products  5.78 us (2%)
    all_gather x2, waiting for transfers between devices, body(): all_rows = lax.all_gather(sending, 'row', axis=0, tiled=True)  152 us
    all_gather x2, blocking collectives, body(): tile_full = lax.all_gather(tile_wide, 'row', axis=0, tiled=True)  94.3 us
    all_gather x2, blocking collectives, body(): tile_wide = lax.all_gather(tile_piece, 'col', axis=1, tiled=True)  41.3 us
    another operation x6, other arithmetic, body(): factor = jnp.tril(jnp.linalg.cholesky(symmetric))  24.9 us
    another operation x4, other arithmetic, solve_rows(): return jax.scipy.linalg.solve_triangular(factor, rows_in.T, lower=True).T  20.8 us
    unnamed x18, local copies, waits for them, and re-layouts  11.1 us
  transfers between devices with their start and end apart: 4, of which 2 were waited for; matrix products, arithmetic and copies ran while one was open for 13% of the time, Pallas kernels for 0%

commit v1 on v0

--- a/solution.py
+++ b/solution.py
@@ -38,7 +38,9 @@
         first_row = panel_step * tile_height
         tile_piece = blocks[first_row : first_row + tile_height, first_col:after_col]
         tile_wide = lax.all_gather(tile_piece, "col", axis=1, tiled=True)
-        tile_full = lax.all_gather(tile_wide, "row", axis=0, tiled=True)
+        tile_full = jnp.concatenate(
+            lax.all_to_all(jnp.stack([tile_wide] * lax.axis_size("row")), "row", 0, 0), axis=0
+        )
         tile_full = tile_full.reshape(row_count, tile_height, NB).transpose(1, 0, 2).reshape(NB, NB)
         diag_tile = unmix_cols(tile_full, col_count)
         symmetric = jnp.tril(diag_tile) + jnp.tril(diag_tile, -1).T

time: 380 us -> 314 us (0.83)
  blocking collectives: 136 us -> 41.3 us
  starting transfers between devices: 0.31 us -> 18.2 us
  waiting for transfers between devices: 152 us -> 161 us
    all_gather x2 -> x0, blocking collectives: 94.3 us -> none  [body(): tile_full = lax.all_gather(tile_wide, 'row', axis=0, tiled=True)]
    all_to_all x0 -> x2, starting transfers between devices: none -> 17.9 us  [body(): lax.all_to_all(jnp.stack([tile_wide] * lax.axis_size('row')), 'row', 0, 0)]
    all_to_all x0 -> x2, waiting for transfers between devices: none -> 15 us  [body(): lax.all_to_all(jnp.stack([tile_wide] * lax.axis_size('row')), 'row', 0, 0)]
    all_gather x2, waiting for transfers between devices: 152 us -> 146 us  [body(): all_rows = lax.all_gather(sending, 'row', axis=0, tiled=True)]
  transfers between devices with their start and end apart: 4 -> 6, of which waited for: 2 -> 4; matrix products, arithmetic and copies ran while one was open for 13% -> 17% of each run, Pallas kernels for 0% -> 0%
where the time goes in v1:
time: 314 us
  waiting for transfers between devices  161 us (51%)
  other arithmetic  47.1 us (15%)
  blocking collectives  41.3 us (13%)
  local copies, waits for them, and re-layouts  27.1 us (9%)
  starting transfers between devices  18.2 us (6%)
  between operations  13.6 us (4%)
  matrix products  5.77 us (2%)
    all_gather x2, waiting for transfers between devices, body(): all_rows = lax.all_gather(sending, 'row', axis=0, tiled=True)  146 us
    all_gather x2, blocking collectives, body(): tile_wide = lax.all_gather(tile_piece, 'col', axis=1, tiled=True)  41.3 us
    another operation x6, other arithmetic, body(): factor = jnp.tril(jnp.linalg.cholesky(symmetric))  24.9 us
    another operation x4, other arithmetic, solve_rows(): return jax.scipy.linalg.solve_triangular(factor, rows_in.T, lower=True).T  20.8 us
    all_to_all x2, starting transfers between devices, body(): lax.all_to_all(jnp.stack([tile_wide] * lax.axis_size('row')), 'row', 0, 0)  17.9 us
    all_to_all x2, waiting for transfers between devices, body(): lax.all_to_all(jnp.stack([tile_wide] * lax.axis_size('row')), 'row', 0, 0)  15 us
    unnamed x18, local copies, waits for them, and re-layouts  11.1 us
  transfers between devices with their start and end apart: 6, of which 4 were waited for; matrix products, arithmetic and copies ran while one was open for 17% of the time, Pallas kernels for 0%

profile of v1, /device:TPU:14, one launch (start us, length us, event | category | flops | bytes accessed | tf_op | source)
XLA Modules:
  0.0 313.7 jit_solution(1317068976124358734)
XLA Ops:
  6.5 4.6 %copy.53 = f32[1,2048,1,256]{1,3,2,0:T(8,128)S(1)} copy(f32[1,2048,1,256]{3,2,1,0:T(1,128)} %param.4) | data formatting | bytes 4194304 | tf_op args[0]
  11.1 0.6 slice.65
  11.9 23.2 %all-gather = f32[16,8,4]{1,2,0:T(4,128)S(1)} all-gather(f32[1,8,4]{1,2,0:T(4,128)S(1)} %bitcast.132), channel_id=1, replica_groups=mesh['row'=32,'col'=16] {'col'}, dimensions={0}, use_global_device_ids=true | all-gather | bytes 2176 | tf_op jit(solution)/shard_map/all_gather | solution.py:40
  35.1 0.1 reshape.167
  35.2 0.6 stack.4
  35.8 10.1 %all-to-all-start = ((f32[32,4,128]{2,1,0:T(4,128)}), f32[32,4,128]{2,1,0:T(4,128)S(1)}, u32[]{:S(2)}, u32[]{:S(2)}) async-start(f32[32,4,128]{2,1,0:T(4,128)} %stack.4), calls=%async_computation | async-start | bytes 131072 | tf_op jit(solution)/shard_map/all_to_all | solution.py:42
  46.0 7.6 %all-to-all-done = f32[32,4,128]{2,1,0:T(4,128)S(1)} async-done(((f32[32,4,128]{2,1,0:T(4,128)}), f32[32,4,128]{2,1,0:T(4,128)S(1)}, u32[]{:S(2)}, u32[]{:S(2)}) %all-to-all-start) | async-done | bytes 65568 | tf_op jit(solution)/shard_map/all_to_all | solution.py:42
  53.6 0.1 copy.56
  53.7 0.2 reshape_reshape.6
  54.0 0.1 bitcast_add_fusion.3
  54.2 11.7 %cholesky.44 = f32[128,128]{1,0:T(8,128)S(1)} custom-call(f32[128,128]{1,0:T(8,128)S(1)} %fusion.8), custom_call_target="Cholesky" | custom-call | tf_op jit(solution)/shard_map/jit(cholesky)/cholesky | solution.py:47
  65.9 0.1 copy.61
  66.0 0.1 select_reduce_fusion.1
  66.1 0.6 compare_reduce_fusion.1
  66.8 0.6 select_bitcast_fusion.1
  67.4 0.1 copy.64
  67.5 0.1 copy.68
  67.7 9.8 %custom-call.6 = f32[1,128,128]{1,2,0:T(8,128)S(1)} custom-call(f32[1,128,128]{2,1,0:T(8,128)S(1)} %copy.65), custom_call_target="InvertDiagBlocksLowerTriangular" | custom-call | tf_op jit(solution)/shard_map/jit(_solve_triangular)/triangular_solve | solution.py:20
  77.5 1.8 copy.66
  79.4 1.1 convolution_bitcast_fusion.1
  80.4 0.3 slice.66
  80.8 0.7 pad_maximum_fusion
  81.5 0.2 all-gather.11.cloned.1.call-start
  81.7 72.9 %all-gather.9.cloned.1.call-done = f32[4096,128]{0,1:T(8,128)} async-done(((f32[128,128]{0,1:T(8,128)}), f32[4096,128]{0,1:T(8,128)}) %all-gather.9.cloned.1.call-update) | async-done | bytes 2097168 | tf_op jit(solution)/shard_map/all_gather | solution.py:62
  154.7 2.0 copy.90
  156.6 0.1 constant_dynamic-slice_fusion.2
  156.8 0.1 copy.69
  156.9 1.9 convolution_subtract_fusion
  158.9 1.3 copy-done
  160.1 0.6 slice.70
  160.8 0.8 slice_bitcast_fusion
  161.6 18.1 %all-gather.1 = f32[16,8,4]{1,2,0:T(4,128)S(1)} all-gather(f32[1,8,4]{1,2,0:T(4,128)S(1)} %bitcast.134), channel_id=1, replica_groups=mesh['row'=32,'col'=16] {'col'}, dimensions={0}, use_global_device_ids=true | all-gather | bytes 2176 | tf_op jit(solution)/shard_map/all_gather | solution.py:40
  179.8 0.1 reshape.169
  179.9 0.6 stack.5
  180.5 7.7 %all-to-all-start.1 = ((f32[32,4,128]{2,1,0:T(4,128)}), f32[32,4,128]{2,1,0:T(4,128)S(1)}, u32[]{:S(2)}, u32[]{:S(2)}) async-start(f32[32,4,128]{2,1,0:T(4,128)} %stack.5), calls=%async_computation.1 | async-start | bytes 131072 | tf_op jit(solution)/shard_map/all_to_all | solution.py:42
  188.3 0.1 copy.77
  188.4 7.4 %all-to-all-done.1 = f32[32,4,128]{2,1,0:T(4,128)S(1)} async-done(((f32[32,4,128]{2,1,0:T(4,128)}), f32[32,4,128]{2,1,0:T(4,128)S(1)}, u32[]{:S(2)}, u32[]{:S(2)}) %all-to-all-start.1) | async-done | bytes 65568 | tf_op jit(solution)/shard_map/all_to_all | solution.py:42
  195.9 0.2 copy.72
  196.0 0.2 reshape_reshape.7
  196.2 0.1 copy.75
  196.3 0.1 bitcast_add_fusion.1
  196.4 0.1 copy.76
  196.5 11.7 %cholesky.55 = f32[128,128]{1,0:T(8,128)S(1)} custom-call(f32[128,128]{1,0:T(8,128)S(1)} %fusion.6), custom_call_target="Cholesky" | custom-call | tf_op jit(solution)/shard_map/jit(cholesky)/cholesky | solution.py:47
  208.2 0.7 compare_reduce_fusion
  208.9 0.6 select_bitcast_fusion
  209.6 9.8 %custom-call.7 = f32[1,128,128]{1,2,0:T(8,128)S(1)} custom-call(f32[1,128,128]{2,1,0:T(8,128)S(1)} %get-tuple-element.6), custom_call_target="InvertDiagBlocksLowerTriangular" | custom-call | tf_op jit(solution)/shard_map/jit(_solve_triangular)/triangular_solve | solution.py:20
  219.4 0.1 copy.82
  219.6 1.8 copy.79
  221.4 1.1 convolution_bitcast_fusion
  222.4 0.3 slice.71
  222.8 1.0 concatenate.45
  223.8 0.7 slice.73
  224.5 0.1 copy.85
  224.6 0.2 fusion.4
  224.9 0.1 copy.80
  225.0 0.6 copy.81
  225.7 0.7 concatenate.43
  226.4 72.6 %all-gather.13.cloned.1.call-done = f32[4096,128]{0,1:T(8,128)} async-done(((f32[128,128]{0,1:T(8,128)}), f32[4096,128]{0,1:T(8,128)}) %all-gather.13.cloned.1.call-update) | async-done | bytes 2097168 | tf_op jit(solution)/shard_map/all_gather | solution.py:62
  299.1 2.1 copy.91
  301.2 0.1 constant_dynamic-slice_fusion
  301.3 0.1 copy.83
  301.6 1.8 fusion
  303.3 0.2 maximum_select_fusion
  303.5 3.6 %copy.84 = f32[1,2048,1,256]{3,2,1,0:T(1,128)} copy(f32[1,2048,1,256]{1,3,2,0:T(8,128)S(1)} %maximum_select_fusion) | data formatting | bytes 4194304 | tf_op jit(solution)/shard_map/jit(_where)/select_n | solution.py:73
  (41 shorter events, 1.0 us)
Async XLA Ops:
  6.5 71.0 %all-gather.7.cloned.1.call-start = ((), (), s32[]{:S(2)}) async-start(), calls=%async_computation.2 | async-start | bytes 1114112 | tf_op jit(solution)/shard_map/all_gather | solution.py:49
  35.8 17.8 %all-to-all-start = ((f32[32,4,128]{2,1,0:T(4,128)}), f32[32,4,128]{2,1,0:T(4,128)S(1)}, u32[]{:S(2)}, u32[]{:S(2)}) async-start(f32[32,4,128]{2,1,0:T(4,128)} %stack.4), calls=%async_computation | async-start | bytes 131072 | tf_op jit(solution)/shard_map/all_to_all | solution.py:42
  45.9 108.7 %all-gather.9.cloned.1.call-start = ((), (), s32[]{:S(2)}) async-start(), calls=%async_computation.3 | async-start | bytes 2162688 | tf_op jit(solution)/shard_map/all_gather | solution.py:62
  81.5 138.0 %all-gather.11.cloned.1.call-start = ((), (), s32[]{:S(2)}) async-start(), calls=%async_computation.4 | async-start | bytes 1114112 | tf_op jit(solution)/shard_map/all_gather | solution.py:49
  158.8 1.3 copy-start
  180.5 15.4 %all-to-all-start.1 = ((f32[32,4,128]{2,1,0:T(4,128)}), f32[32,4,128]{2,1,0:T(4,128)S(1)}, u32[]{:S(2)}, u32[]{:S(2)}) async-start(f32[32,4,128]{2,1,0:T(4,128)} %stack.5), calls=%async_computation.1 | async-start | bytes 131072 | tf_op jit(solution)/shard_map/all_to_all | solution.py:42
  188.2 110.9 %all-gather.13.cloned.1.call-start = ((), (), s32[]{:S(2)}) async-start(), calls=%async_computation.5 | async-start | bytes 2162688 | tf_op jit(solution)/shard_map/all_gather | solution.py:62
  223.8 2.6 copy-start.2
  299.1 2.4 copy-start.1
  299.1 2.5 copy-start.3
Sparse Core Ops, SparseCore 0:
  11.9 46.4 all-gather.6
  81.6 73.0 all-gather.8
  160.9 41.1 all-gather.10
  224.6 74.4 all-gather.12
